TPU v7x, 32 devices: a whole 2x2x4 slice. The times are simulated.
32 devices in a mesh: roll: 4 (over y, x), seq: 8 (over z, core).
Axes of the slice: x: 2, y: 2, z: 4, core: 2. Of those that a mesh axis runs over, the one named last changes fastest.
Arguments:
- query_rows: bfloat16 [4, 4096, 1792], P('roll', 'seq'), may hold values from -200 to 200
- key_rows: bfloat16 [4, 4096, 256], P('roll', 'seq'), may hold values from -6 to 6
- value_rows: bfloat16 [4, 4096, 256], P('roll', 'seq'), may hold values from -6 to 6
- cotangent: bfloat16 [4, 4096, 1792], P('roll', None, 'seq'), may hold values from -6 to 6
- slopes: float32 [14], replicated, may hold values from 0.00029296876 to 0.0390625
- lengths: int32 [4], P('roll'), may hold values from 1024 to 4096, as said below
- loss_mask: int32 [4, 4096], P('roll', 'seq'), may hold values 0 or 1
- distances: int32 [4], P('roll'), may hold values from 40 to 357
Outputs:
- grad_queries: bfloat16 [4, 4096, 1792], P('roll', 'seq')
- grad_keys: bfloat16 [4, 4096, 256], P('roll', 'seq')
- grad_values: bfloat16 [4, 4096, 256], P('roll', 'seq')
Inputs may be any that keep to these rules, and one draw needn't show every extreme that they name: `lengths`: some rollout has 4096 tokens and some 4096 // 4.
All inputs are finite; a program needn't handle non-finite values. No bound on the sum of `loss_mask` on one device may be relied on, other than what follows from the above.
Results may differ from a plain program's by a relative error of at most 0.0068.
Values may be sent and summed in bfloat16 or wider, within the bound.
No kernel may reach another device: no remote copies, remote signals or barrier semaphores. Data moves between devices by JAX's collectives and lax.ppermute only.
A program may use at most 64 MiB of HBM per device.

v0:
```python
import math
import jax
import jax.numpy as jnp
from jax import lax
from jax.sharding import PartitionSpec as P

HEAD_DIM = 128
WINDOW = 1024


def passed_along(value, axis, steps):
    count = lax.axis_size(axis)
    leading, last = (max(0, -steps), min(count, count - steps))
    return lax.ppermute(value, axis, [(source, source + steps) for source in range(leading, last)])


def shards(query_rows, key_rows, value_rows, cotangent, slopes, lengths, loss_mask, distances):
    own_q = query_rows[0]
    own_k = key_rows[0]
    own_v = value_rows[0]
    tok_rows = own_q.shape[0]
    features = own_q.shape[1]
    kv_features = own_k.shape[1]
    head_dim = HEAD_DIM
    head_count = features // head_dim
    kv_count = kv_features // head_dim
    group_size = head_count // kv_count
    band_reach = (WINDOW - 2) // tok_rows + 1
    band_len = (band_reach + 1) * tok_rows
    seq_len = tok_rows * lax.axis_size("seq")
    seq_pos = lax.axis_index("seq")
    attn_scale = 1.0 / math.sqrt(head_dim)
    positions = seq_pos * tok_rows + jnp.arange(tok_rows, dtype=jnp.int32)
    valid = ((positions < lengths[0]) & (loss_mask[0] == 1)).astype(jnp.float32)
    local_count = jnp.sum(valid)
    my_distance = distances[0].astype(jnp.float32)
    count_all = lax.psum(local_count, "seq")
    group_total = lax.psum(my_distance, "roll")
    advantage = (group_total / lax.axis_size("roll") - my_distance) / 64.0
    weight = advantage * valid * seq_len / (1.0 + count_all)
    arrived = lax.all_to_all(cotangent, "seq", split_axis=1, concat_axis=2, tiled=True)[0]
    dout = (arrived.astype(jnp.float32) * weight[:, None]).astype(jnp.bfloat16)
    kv_pair = jnp.stack([own_k, own_v])
    earlier = []
    for offset in range(1, band_reach + 1):
        earlier.append(passed_along(kv_pair, "seq", offset))
    ordered = earlier[::-1]
    band_k = jnp.concatenate([blk[0] for blk in ordered] + [own_k], 0)
    band_v = jnp.concatenate([blk[1] for blk in ordered] + [own_v], 0)
    key_pos = (seq_pos - band_reach) * tok_rows + jnp.arange(band_len, dtype=jnp.int32)
    pos_gap = positions[:, None] - key_pos[None, :]
    allowed = (pos_gap >= 0) & (pos_gap < WINDOW) & (key_pos[None, :] >= 0)
    gap_float = pos_gap.astype(jnp.float32)
    split_at = band_reach * tok_rows
    contract_rows = (((0,), (0,)), ((), ()))

    def head_step(head, carry):
        grad_q, own_dk, own_dv, part_k, part_v = carry
        column = head * head_dim
        kv_column = head // group_size * head_dim
        q_head = lax.dynamic_slice_in_dim(own_q, column, head_dim, 1)
        k_head = lax.dynamic_slice_in_dim(band_k, kv_column, head_dim, 1)
        v_head = lax.dynamic_slice_in_dim(band_v, kv_column, head_dim, 1)
        d_head = lax.dynamic_slice_in_dim(dout, column, head_dim, 1)
        slope = lax.dynamic_index_in_dim(slopes, head, keepdims=False)
        scores = (
            jnp.dot(q_head, k_head.T, preferred_element_type=jnp.float32) * attn_scale
            - slope * gap_float
        )
        masked = jnp.where(allowed, scores, -jnp.inf)
        row_max = jnp.max(masked, axis=1, keepdims=True)
        exp_terms = jnp.where(allowed, jnp.exp(masked - row_max), 0.0)
        probs = exp_terms / jnp.sum(exp_terms, axis=1, keepdims=True)
        probs_low = probs.astype(jnp.bfloat16)
        dprob = jnp.dot(d_head, v_head.T, preferred_element_type=jnp.float32)
        row_delta = jnp.sum(probs * dprob, axis=1, keepdims=True)
        dscore = (probs * (dprob - row_delta) * attn_scale).astype(jnp.bfloat16)
        head_dq = jnp.dot(dscore, k_head, preferred_element_type=jnp.float32).astype(jnp.bfloat16)
        band_dk = lax.dot_general(dscore, q_head, contract_rows, preferred_element_type=jnp.float32)
        band_dv = lax.dot_general(
            probs_low, d_head, contract_rows, preferred_element_type=jnp.float32
        )
        grad_q = lax.dynamic_update_slice_in_dim(grad_q, head_dq, column, 1)
        own_dk = lax.dynamic_update_slice_in_dim(
            own_dk,
            lax.dynamic_slice_in_dim(own_dk, kv_column, head_dim, 1) + band_dk[split_at:],
            kv_column,
            1,
        )
        own_dv = lax.dynamic_update_slice_in_dim(
            own_dv,
            lax.dynamic_slice_in_dim(own_dv, kv_column, head_dim, 1) + band_dv[split_at:],
            kv_column,
            1,
        )
        far_dk = band_dk[:split_at].reshape(band_reach, tok_rows, head_dim)
        far_dv = band_dv[:split_at].reshape(band_reach, tok_rows, head_dim)
        part_k = lax.dynamic_update_slice_in_dim(
            part_k, lax.dynamic_slice_in_dim(part_k, kv_column, head_dim, 2) + far_dk, kv_column, 2
        )
        part_v = lax.dynamic_update_slice_in_dim(
            part_v, lax.dynamic_slice_in_dim(part_v, kv_column, head_dim, 2) + far_dv, kv_column, 2
        )
        return (grad_q, own_dk, own_dv, part_k, part_v)

    start_carry = (
        jnp.zeros((tok_rows, features), jnp.bfloat16),
        jnp.zeros((tok_rows, kv_features), jnp.float32),
        jnp.zeros((tok_rows, kv_features), jnp.float32),
        jnp.zeros((band_reach, tok_rows, kv_features), jnp.float32),
        jnp.zeros((band_reach, tok_rows, kv_features), jnp.float32),
    )
    grad_q, total_k, total_v, part_k, part_v = lax.fori_loop(0, head_count, head_step, start_carry)
    part_k = part_k.astype(jnp.bfloat16)
    part_v = part_v.astype(jnp.bfloat16)
    for offset in range(1, band_reach + 1):
        outgoing = jnp.stack([part_k[band_reach - offset], part_v[band_reach - offset]])
        incoming = passed_along(outgoing, "seq", -offset)
        total_k = total_k + incoming[0].astype(jnp.float32)
        total_v = total_v + incoming[1].astype(jnp.float32)
    return (grad_q[None], total_k.astype(jnp.bfloat16)[None], total_v.astype(jnp.bfloat16)[None])


def solution(mesh):
    placed = (
        P("roll", "seq", None),
        P("roll", "seq", None),
        P("roll", "seq", None),
        P("roll", None, "seq"),
        P(),
        P("roll"),
        P("roll", "seq"),
        P("roll"),
    )
    return jax.shard_map(
        shards,
        mesh=mesh,
        in_specs=placed,
        out_specs=(P("roll", "seq", None), P("roll", "seq", None), P("roll", "seq", None)),
        check_vma=False,
    )
```

profile of v0, /device:TPU:19, one launch (start us, length us, event | category | flops | bytes accessed | tf_op | source)
XLA Modules:
  0.0 346.7 jit_solution(13123298232539514425)
XLA Ops:
  0.6 10.0 %copy.19 = bf16[1,4096,224]{2,0,1:T(2,128)(2,1)} copy(bf16[1,4096,224]{1,2,0:T(8,128)(2,1)} %param.13) | data formatting | bytes 3670016 | tf_op args[3]
  11.1 23.6 %reduce.2 = bf16[4096,224]{1,0:T(8,128)(2,1)S(1)} reduce(bf16[4096,1,224]{2,1,0:T(2,128)(2,1)} %bitcast.71, bf16[]{:T(256)} %broadcast.76), dimensions={1}, to_apply=%bitcast.53.reduce_sub_computation | reduce | bytes 3670018
  34.8 5.2 %reshape.80 = bf16[8,2,57344]{2,1,0:T(2,128)(2,1)} reshape(bf16[4096,224]{1,0:T(8,128)(2,1)S(1)} %reduce.2) | data formatting | bytes 3670016
  40.0 5.7 %all-to-all-start = ((bf16[8,2,57344]{2,1,0:T(2,128)(2,1)}), bf16[8,2,57344]{2,1,0:T(2,128)(2,1)S(1)}, u32[]{:S(2)}, u32[]{:S(2)}) async-start(bf16[8,2,57344]{2,1,0:T(2,128)(2,1)} %reshape.80), calls=%async_computation | async-start | bytes 3670016 | tf_op jit(solution)/shard_map/all_to_all | solution.py:41
  47.1 3.3 collective-permute-start.1
  54.3 7.8 %psum.14 = f32[]{:T(128)} all-reduce(f32[]{:T(128)} %bitcast.7), channel_id=1, replica_groups=mesh['roll'=4,'seq'=8] {'roll'}, use_global_device_ids=true, to_apply=%region_0.0 | all-reduce | flops 1 | bytes 8 | tf_op jit(solution)/shard_map/psum | solution.py:38
  62.0 47.4 %psum.15 = f32[]{:T(128)} all-reduce(f32[]{:T(128)} %convert_reduce_fusion), channel_id=1, replica_groups=mesh['roll'=4,'seq'=8] {'seq'}, use_global_device_ids=true, to_apply=%region_2.0 | all-reduce | flops 1 | bytes 8 | tf_op jit(solution)/shard_map/psum | solution.py:37
  113.1 5.8 %reshape.81 = bf16[4096,1,224]{2,1,0:T(2,128)(2,1)} reshape(bf16[8,2,57344]{2,1,0:T(2,128)(2,1)S(1)} %all-to-all-done) | data formatting | bytes 3670016
  118.9 10.1 %copy.20 = bf16[1,4096,224]{1,2,0:T(8,128)(2,1)S(1)} copy(bf16[1,4096,224]{2,0,1:T(2,128)(2,1)} %bitcast.72) | data formatting | bytes 3670016 | tf_op jit(solution)/shard_map/all_to_all | solution.py:41
  129.5 3.3 copy.24
  138.3 186.0 %while.25 = (s32[]{:T(128)}, bf16[512,1792]{1,0:T(8,128)(2,1)}, f32[512,256]{1,0:T(8,128)S(1)}, f32[512,256]{1,0:T(8,128)S(1)}, f32[2,512,256]{2,1,0:T(8,128)S(1...) while((s32[]{:T(128)}, bf16[512,1792]{1,0:T(8,128)(2,1)}, ...), condition=%wide.region_7.8_spmd.clone.clone, body=%wide.region_3.7_spmd.clone.clone.sunk | while | flops 1033828864 | bytes 46446556 | solution.py:113
  138.8 3.3 fusion.59
  152.1 3.3 fusion.59
  165.4 3.3 fusion.59
  178.6 3.3 fusion.59
  191.9 3.3 fusion.59
  205.2 3.3 fusion.59
  218.4 3.3 fusion.59
  231.7 3.3 fusion.59
  236.3 2.8 multiply_reduce_fusion.2
  245.0 3.3 fusion.59
  249.7 2.8 multiply_reduce_fusion.2
  258.3 3.3 fusion.59
  263.0 2.8 multiply_reduce_fusion.2
  271.7 3.3 fusion.59
  276.3 2.8 multiply_reduce_fusion.2
  285.0 3.3 fusion.59
  289.6 2.8 multiply_reduce_fusion.2
  298.3 3.3 fusion.59
  311.6 3.3 fusion.59
  328.7 11.2 %collective-permute-done.3 = bf16[2,512,256]{2,1,0:T(8,128)(2,1)S(1)} collective-permute-done((bf16[2,512,256]{2,1,0:T(8,128)(2,1)S(1)}, bf16[2,512,256]{2,1,0:T(8,128)(2,1)S(1)}, u32[]{:S(2)}, u32[]{:S(2)}) %collective-permute-start.3) | collective-permute-done | bytes 524320 | tf_op jit(solution)/shard_map/ppermute | solution.py:14
  339.9 5.9 %collective-permute-done.2 = bf16[2,512,256]{2,1,0:T(8,128)(2,1)S(1)} collective-permute-done((bf16[2,512,256]{2,1,0:T(8,128)(2,1)S(1)}, bf16[2,512,256]{2,1,0:T(8,128)(2,1)S(1)}, u32[]{:S(2)}, u32[]{:S(2)}) %collective-permute-start.2) | collective-permute-done | bytes 524320 | tf_op jit(solution)/shard_map/ppermute | solution.py:14
  (246 shorter events, 142.8 us)
Async XLA Ops:
  34.7 10.9 %copy-start.1 = (bf16[1,512,256]{2,1,0:T(8,128)(2,1)S(1)}, bf16[1,512,256]{2,1,0:T(8,128)(2,1)}, u32[]{:S(2)}) copy-start(bf16[1,512,256]{2,1,0:T(8,128)(2,1)} %param.11) | copy-start | bytes 786436
  34.8 11.6 %copy-start.2 = (bf16[1,512,256]{2,1,0:T(8,128)(2,1)S(1)}, bf16[1,512,256]{2,1,0:T(8,128)(2,1)}, u32[]{:S(2)}) copy-start(bf16[1,512,256]{2,1,0:T(8,128)(2,1)} %param.12) | copy-start | bytes 786436
  40.0 13.7 %copy-start.4 = (s32[1,512]{1,0:T(1,128)S(1)}, s32[1,512]{1,0:T(1,128)}, u32[]{:S(2)}) copy-start(s32[1,512]{1,0:T(1,128)} %param.16) | copy-start | bytes 6148
  40.0 73.2 %all-to-all-start = ((bf16[8,2,57344]{2,1,0:T(2,128)(2,1)}), bf16[8,2,57344]{2,1,0:T(2,128)(2,1)S(1)}, u32[]{:S(2)}, u32[]{:S(2)}) async-start(bf16[8,2,57344]{2,1,0:T(2,128)(2,1)} %reshape.80), calls=%async_computation | async-start | bytes 3670016 | tf_op jit(solution)/shard_map/all_to_all | solution.py:41
  47.1 63.7 %collective-permute-start.1 = (bf16[2,512,256]{2,1,0:T(8,128)(2,1)}, bf16[2,512,256]{2,1,0:T(8,128)(2,1)}, u32[]{:S(2)}, u32[]{:S(2)}) collective-permute-start(bf16[2,512,256]{2,1,0:T(8,128)(2,1)} %constant_dynamic-update-slice_fusion), channel_id=1, source_target_pairs={{0,1},{1,2},{2,3},{3,4},{4,5},{5,6},{6,7},{8,9},{9,10},{10,11},{11... | collective-permute-start | bytes 1572872 | tf_op jit(solution)/shard_map/ppermute | solution.py:14
  50.4 61.4 %collective-permute-start = (bf16[2,512,256]{2,1,0:T(8,128)(2,1)}, bf16[2,512,256]{2,1,0:T(8,128)(2,1)S(1)}, u32[]{:S(2)}, u32[]{:S(2)}) collective-permute-start(bf16[2,512,256]{2,1,0:T(8,128)(2,1)} %constant_dynamic-update-slice_fusion), channel_id=1, source_target_pairs={{0,2},{1,3},{2,4},{3,5},{4,6},{5,7},{8,10},{9,11},{10,12},{11,13},... | collective-permute-start | bytes 1572872 | tf_op jit(solution)/shard_map/ppermute | solution.py:14
  136.7 1.6 copy-start.5
  142.1 1.4 copy-start.3
  146.7 3.2 copy-start
  155.4 1.4 copy-start.3
  160.0 3.2 copy-start
  168.6 1.4 copy-start.3
  173.2 3.2 copy-start
  181.9 1.4 copy-start.3
  186.5 3.2 copy-start
  195.2 1.4 copy-start.3
  199.8 3.2 copy-start
  208.4 1.4 copy-start.3
  213.0 3.2 copy-start
  221.7 1.4 copy-start.3
  226.3 3.2 copy-start
  235.0 1.4 copy-start.3
  239.6 3.2 copy-start
  248.3 1.4 copy-start.3
  252.9 3.2 copy-start
  266.2 3.2 copy-start
  279.5 3.2 copy-start
  292.8 3.2 copy-start
  306.2 3.2 copy-start
  319.5 3.2 copy-start
  324.6 15.3 %collective-permute-start.3 = (bf16[2,512,256]{2,1,0:T(8,128)(2,1)S(1)}, bf16[2,512,256]{2,1,0:T(8,128)(2,1)S(1)}, u32[]{:S(2)}, u32[]{:S(2)}) collective-permute-start(bf16[2,512,256]{2,1,0:T(8,128)(2,1)S(1)} %pad_maximum_fusion.3), channel_id=1, source_target_pairs={{2,0},{3,1},{4,2},{5,3},{6,4},{7,5},{10,8},{11,9},{12,10},{13,11},... | collective-permute-start | bytes 1572872 | tf_op jit(solution)/shard_map/ppermute | solution.py:14
  326.6 19.2 %collective-permute-start.2 = (bf16[2,512,256]{2,1,0:T(8,128)(2,1)S(1)}, bf16[2,512,256]{2,1,0:T(8,128)(2,1)S(1)}, u32[]{:S(2)}, u32[]{:S(2)}) collective-permute-start(bf16[2,512,256]{2,1,0:T(8,128)(2,1)S(1)} %pad_maximum_fusion.2), channel_id=1, source_target_pairs={{1,0},{2,1},{3,2},{4,3},{5,4},{6,5},{7,6},{9,8},{10,9},{11,10},{12... | collective-permute-start | bytes 1572872 | tf_op jit(solution)/shard_map/ppermute | solution.py:14
  (5 other events, 6.9 us)
where the time goes:
time: 349 us; the launch traced here: 347 us
  matrix products  146 us (42%)
  other arithmetic  58.4 us (17%)
  blocking collectives  55.2 us (16%)
  local copies, waits for them, and re-layouts  50.5 us (14%)
  waiting for transfers between devices  17.1 us (5%)
  starting transfers between devices  14.9 us (4%)
    psum x1, blocking collectives, shards(): count_all = lax.psum(local_count, 'seq')  47.4 us
    dot_general x14, matrix products, head_step(): jnp.dot(q_head, k_head.T, preferred_element_type=jnp.float32) * attn_scale  45.8 us
    dot_general x14, matrix products, head_step(): dprob = jnp.dot(d_head, v_head.T, preferred_element_type=jnp.float32)  38.8 us
    unnamed x14, local copies, waits for them, and re-layouts  25.4 us
    unnamed x1, other arithmetic  23.6 us
    dot_general x14, matrix products, head_step(): lax.dot_general(probs_low, d_head, contract_rows, preferred_element_type=...  22.3 us
    dot_general x14, matrix products, head_step(): lax.dot_general(dscore, q_head, contract_rows, preferred_element_type=jnp...  21.3 us
    reduce_sum x14, other arithmetic, head_step(): probs = exp_terms / jnp.sum(exp_terms, axis=1, keepdims=True)  19.1 us
  transfers between devices with their start and end apart: 5, of which 2 were waited for; matrix products, arithmetic and copies ran while one was open for 1% of the time, Pallas kernels for 0%

commit v1 on v0

--- a/solution.py
+++ b/solution.py
@@ -6,6 +6,39 @@
 
 HEAD_DIM = 128
 WINDOW = 1024
+
+
+def carry_fields_by_axis(state, where_dim, frame):
+    long_array = state.shape
+    seen_now = state.reshape(
+        *long_array[:where_dim], frame, long_array[where_dim] // frame, *long_array[where_dim + 1 :]
+    )
+    return jnp.moveaxis(seen_now, where_dim, 0)
+
+
+def settle_pipes(mine_x, dim_no):
+    mine_x = jnp.moveaxis(mine_x, 0, dim_no)
+    far_arr = mine_x.shape
+    return mine_x.reshape(
+        *far_arr[:dim_no], far_arr[dim_no] * far_arr[dim_no + 1], *far_arr[dim_no + 2 :]
+    )
+
+
+def process_fields(array_here, chip_axis, slab_in, view):
+    s_next = lax.axis_size(chip_axis)
+    piece_now = lax.axis_index(chip_axis)
+    d_next, front = (s_next, piece_now)
+    parts_out = carry_fields_by_axis(array_here, slab_in, d_next)
+    sheets = [parts_out[front]]
+    num = 1
+    while num < d_next:
+        shaped = parts_out[front ^ num]
+        sheets.append(
+            lax.ppermute(shaped, axis_name=chip_axis, perm=[(it, it ^ num) for it in range(d_next)])
+        )
+        num = num + 1
+    parts_out = jnp.stack(sheets, axis=0)[front ^ jnp.arange(d_next)]
+    return settle_pipes(parts_out, view)
 
 
 def passed_along(value, axis, steps):
@@ -38,7 +71,7 @@
     group_total = lax.psum(my_distance, "roll")
     advantage = (group_total / lax.axis_size("roll") - my_distance) / 64.0
     weight = advantage * valid * seq_len / (1.0 + count_all)
-    arrived = lax.all_to_all(cotangent, "seq", split_axis=1, concat_axis=2, tiled=True)[0]
+    arrived = process_fields(cotangent, "seq", 1, 2)[0]
     dout = (arrived.astype(jnp.float32) * weight[:, None]).astype(jnp.bfloat16)
     kv_pair = jnp.stack([own_k, own_v])
     earlier = []

time: 349 us -> 316 us (0.905)
  blocking collectives: 55.2 us -> 19.5 us
  waiting for transfers between devices: 17.1 us -> 50.6 us
  other arithmetic: 58.4 us -> 34.9 us
  local copies, waits for them, and re-layouts: 50.5 us -> 35.2 us
  starting transfers between devices: 14.9 us -> 20.7 us
    psum x1, blocking collectives: 47.4 us -> 12 us  [shards(): count_all = lax.psum(local_count, 'seq')]
    ppermute x0 -> x7, waiting for transfers between devices: none -> 34.2 us  [process_fields(): lax.ppermute(shaped, axis_name=chip_axis, perm=[(it, it ^ num) for it in...]
    unnamed x1 -> x0, other arithmetic: 23.6 us -> none
    unnamed x14 -> x30, local copies, waits for them, and re-layouts: 25.4 us -> 13.6 us
    ppermute x0 -> x7, starting transfers between devices: none -> 10.3 us  [process_fields(): lax.ppermute(shaped, axis_name=chip_axis, perm=[(it, it ^ num) for it in...]
    all_to_all x1 -> x0, local copies, waits for them, and re-layouts: 10.1 us -> none  [shards(): lax.all_to_all(cotangent, 'seq', split_axis=1, concat_axis=2, tiled=True)[0]]
    all_to_all x1 -> x0, starting transfers between devices: 5.66 us -> none  [shards(): lax.all_to_all(cotangent, 'seq', split_axis=1, concat_axis=2, tiled=True)[0]]
    dynamic_slice x0 -> x1, local copies, waits for them, and re-layouts: none -> 4.6 us  [process_fields(): shaped = parts_out[front ^ num]]
  transfers between devices with their start and end apart: 5 -> 11, of which waited for: 2 -> 6; matrix products, arithmetic and copies ran while one was open for 1% -> 7% of each run, Pallas kernels for 0% -> 0%
where the time goes in v1:
time: 316 us; the launch traced here: 312 us
  matrix products  146 us (46%)
  waiting for transfers between devices  50.6 us (16%)
  local copies, waits for them, and re-layouts  35.2 us (11%)
  other arithmetic  34.9 us (11%)
  starting transfers between devices  20.7 us (7%)
  blocking collectives  19.5 us (6%)
  between operations  3.53 us (1%)
    dot_general x14, matrix products, head_step(): jnp.dot(q_head, k_head.T, preferred_element_type=jnp.float32) * attn_scale  45.8 us
    dot_general x14, matrix products, head_step(): dprob = jnp.dot(d_head, v_head.T, preferred_element_type=jnp.float32)  38.8 us
    ppermute x7, waiting for transfers between devices, process_fields(): lax.ppermute(shaped, axis_name=chip_axis, perm=[(it, it ^ num) for it in...  34.2 us
    dot_general x14, matrix products, head_step(): lax.dot_general(dscore, q_head, contract_rows, preferred_element_type=jnp...  22.2 us
    dot_general x14, matrix products, head_step(): lax.dot_general(probs_low, d_head, contract_rows, preferred_element_type=...  21.3 us
    reduce_sum x14, other arithmetic, head_step(): probs = exp_terms / jnp.sum(exp_terms, axis=1, keepdims=True)  19.1 us
    dot_general x14, matrix products, head_step(): jnp.dot(dscore, k_head, preferred_element_type=jnp.float32)  17.4 us
    ppermute x4, waiting for transfers between devices, passed_along(): lax.ppermute(value, axis, [(source, source + steps) for source in range(l...  16.4 us
  transfers between devices with their start and end apart: 11, of which 6 were waited for; matrix products, arithmetic and copies ran while one was open for 7% of the time, Pallas kernels for 0%

profile of v1, /device:TPU:19, one launch (start us, length us, event | category | flops | bytes accessed | tf_op | source)
XLA Modules:
  0.0 311.6 jit_solution(8846768048664474882)
XLA Ops:
  4.0 3.8 %collective-permute-start.1 = (bf16[2,512,256]{2,1,0:T(8,128)(2,1)}, bf16[2,512,256]{2,1,0:T(8,128)(2,1)}, u32[]{:S(2)}, u32[]{:S(2)}) collective-permute-start(bf16[2,512,256]{2,1,0:T(8,128)(2,1)} %constant_dynamic-update-slice_fusion), channel_id=1, source_target_pairs={{0,1},{1,2},{2,3},{3,4},{4,5},{5,6},{6,7},{8,9},{9,10},{10,11},{11... | collective-permute-start | bytes 1572872 | tf_op jit(solution)/shard_map/ppermute | solution.py:47
  12.0 4.6 %constant_dynamic-slice_fusion = (bf16[1,1,512,224]{2,0,3,1:T(2,128)(2,1)}, bf16[1,1,512,224]{2,0,3,1:T(2,128)(2,1)S(1)}, bf16[1,1,512,224]{2,0,3,1:T(2,128)(2,1...) fusion(bf16[8,1,512,224]{2,0,3,1:T(8,128)(2,1)S(1)} %bitcast.12, ...), kind=kLoop, calls=%fused_computation.89 | loop fusion | bytes 3670048 | tf_op jit(solution)/shard_map/dynamic_slice | solution.py:35
  24.0 7.5 %psum.14 = f32[]{:T(128)} all-reduce(f32[]{:T(128)} %bitcast.24), channel_id=1, replica_groups=mesh['roll'=4,'seq'=8] {'roll'}, use_global_device_ids=true, to_apply=%region_0.0 | all-reduce | flops 1 | bytes 8 | tf_op jit(solution)/shard_map/psum | solution.py:71
  31.5 12.0 %psum.15 = f32[]{:T(128)} all-reduce(f32[]{:T(128)} %convert_reduce_fusion), channel_id=1, replica_groups=mesh['roll'=4,'seq'=8] {'seq'}, use_global_device_ids=true, to_apply=%region_2.0 | all-reduce | flops 1 | bytes 8 | tf_op jit(solution)/shard_map/psum | solution.py:70
  48.0 5.4 %collective-permute-start.5 = (bf16[1,512,224]{1,2,0:T(8,128)(2,1)S(1)}, bf16[1,512,224]{1,2,0:T(8,128)(2,1)S(1)}, u32[]{:S(2)}, u32[]{:S(2)}) collective-permute-start(bf16[1,512,224]{1,2,0:T(8,128)(2,1)S(1)} %bitcast.134), channel_id=1, source_target_pairs={{0,4},{1,5},{2,6},{3,7},{4,0},{5,1},{6,2},{7,3},{8,12},{9,13},{10,... | collective-permute-start | bytes 688136 | tf_op jit(solution)/shard_map/ppermute | solution.py:37
  56.0 14.8 %collective-permute-done.5 = bf16[1,512,224]{1,2,0:T(8,128)(2,1)S(1)} collective-permute-done((bf16[1,512,224]{1,2,0:T(8,128)(2,1)S(1)}, bf16[1,512,224]{1,2,0:T(8,128)(2,1)S(1)}, u32[]{:S(2)}, u32[]{:S(2)}) %collective-permute-start.5) | collective-permute-done | bytes 229408 | tf_op jit(solution)/shard_map/ppermute | solution.py:37
  72.9 2.9 collective-permute-done.6
  75.8 11.6 %collective-permute-done.7 = bf16[1,512,224]{1,2,0:T(8,128)(2,1)S(1)} collective-permute-done((bf16[1,512,224]{1,2,0:T(8,128)(2,1)S(1)}, bf16[1,512,224]{1,2,0:T(8,128)(2,1)S(1)}, u32[]{:S(2)}, u32[]{:S(2)}) %collective-permute-start.7) | collective-permute-done | bytes 229408 | tf_op jit(solution)/shard_map/ppermute | solution.py:37
  87.5 4.9 %collective-permute-done.8 = bf16[1,512,224]{1,2,0:T(8,128)(2,1)S(1)} collective-permute-done((bf16[1,512,224]{1,2,0:T(8,128)(2,1)S(1)}, bf16[1,512,224]{1,2,0:T(8,128)(2,1)S(1)}, u32[]{:S(2)}, u32[]{:S(2)}) %collective-permute-start.8) | collective-permute-done | bytes 229408 | tf_op jit(solution)/shard_map/ppermute | solution.py:37
  103.2 186.0 %while.25 = (s32[]{:T(128)}, bf16[512,1792]{1,0:T(8,128)(2,1)}, f32[512,256]{1,0:T(8,128)S(1)}, f32[512,256]{1,0:T(8,128)S(1)}, f32[2,512,256]{2,1,0:T(8,128)S(1...) while((s32[]{:T(128)}, bf16[512,1792]{1,0:T(8,128)(2,1)}, ...), condition=%wide.region_7.8_spmd.clone.clone, body=%wide.region_3.7_spmd.clone.clone.sunk | while | flops 1033828864 | bytes 46446556 | solution.py:146
  103.8 3.3 %fusion.60 = (f32[512]{0:T(512)S(1)}, f32[512,1536]{1,0:T(8,128)S(1)}) fusion(f32[]{:T(128)} %bitcast.117, bf16[1536,256]{1,0:T(8,128)(2,1)} %get-tuple-element.633, s32[]{:T(128)S(6)} %select_n.143, bf16[512,1792]{1,0:T(8,128)(2,1)} %get-tuple-element.632, s32[]{:T(128)S(6)} %select_n.141, pred[1536]{0:T(1024)(128)(4,1)S(1)} %get-tuple-element.639, ...), kind=kOutput, calls=%fused_computation.99.clone.1 | convolution fusion | flops 209976832 | bytes 3682312 | tf_op jit(solution)/shard_map/while/body/eval_jaxpr/dot_general | solution.py:100
  117.1 3.3 %fusion.60 = (f32[512]{0:T(512)S(1)}, f32[512,1536]{1,0:T(8,128)S(1)}) fusion(f32[]{:T(128)} %bitcast.117, bf16[1536,256]{1,0:T(8,128)(2,1)} %get-tuple-element.633, s32[]{:T(128)S(6)} %select_n.143, bf16[512,1792]{1,0:T(8,128)(2,1)} %get-tuple-element.632, s32[]{:T(128)S(6)} %select_n.141, pred[1536]{0:T(1024)(128)(4,1)S(1)} %get-tuple-element.639, ...), kind=kOutput, calls=%fused_computation.99.clone.1 | convolution fusion | flops 209976832 | bytes 3682312 | tf_op jit(solution)/shard_map/while/body/eval_jaxpr/dot_general | solution.py:100
  130.3 3.3 %fusion.60 = (f32[512]{0:T(512)S(1)}, f32[512,1536]{1,0:T(8,128)S(1)}) fusion(f32[]{:T(128)} %bitcast.117, bf16[1536,256]{1,0:T(8,128)(2,1)} %get-tuple-element.633, s32[]{:T(128)S(6)} %select_n.143, bf16[512,1792]{1,0:T(8,128)(2,1)} %get-tuple-element.632, s32[]{:T(128)S(6)} %select_n.141, pred[1536]{0:T(1024)(128)(4,1)S(1)} %get-tuple-element.639, ...), kind=kOutput, calls=%fused_computation.99.clone.1 | convolution fusion | flops 209976832 | bytes 3682312 | tf_op jit(solution)/shard_map/while/body/eval_jaxpr/dot_general | solution.py:100
  143.6 3.3 %fusion.60 = (f32[512]{0:T(512)S(1)}, f32[512,1536]{1,0:T(8,128)S(1)}) fusion(f32[]{:T(128)} %bitcast.117, bf16[1536,256]{1,0:T(8,128)(2,1)} %get-tuple-element.633, s32[]{:T(128)S(6)} %select_n.143, bf16[512,1792]{1,0:T(8,128)(2,1)} %get-tuple-element.632, s32[]{:T(128)S(6)} %select_n.141, pred[1536]{0:T(1024)(128)(4,1)S(1)} %get-tuple-element.639, ...), kind=kOutput, calls=%fused_computation.99.clone.1 | convolution fusion | flops 209976832 | bytes 3682312 | tf_op jit(solution)/shard_map/while/body/eval_jaxpr/dot_general | solution.py:100
  156.8 3.3 %fusion.60 = (f32[512]{0:T(512)S(1)}, f32[512,1536]{1,0:T(8,128)S(1)}) fusion(f32[]{:T(128)} %bitcast.117, bf16[1536,256]{1,0:T(8,128)(2,1)} %get-tuple-element.633, s32[]{:T(128)S(6)} %select_n.143, bf16[512,1792]{1,0:T(8,128)(2,1)} %get-tuple-element.632, s32[]{:T(128)S(6)} %select_n.141, pred[1536]{0:T(1024)(128)(4,1)S(1)} %get-tuple-element.639, ...), kind=kOutput, calls=%fused_computation.99.clone.1 | convolution fusion | flops 209976832 | bytes 3682312 | tf_op jit(solution)/shard_map/while/body/eval_jaxpr/dot_general | solution.py:100
  170.1 3.3 %fusion.60 = (f32[512]{0:T(512)S(1)}, f32[512,1536]{1,0:T(8,128)S(1)}) fusion(f32[]{:T(128)} %bitcast.117, bf16[1536,256]{1,0:T(8,128)(2,1)} %get-tuple-element.633, s32[]{:T(128)S(6)} %select_n.143, bf16[512,1792]{1,0:T(8,128)(2,1)} %get-tuple-element.632, s32[]{:T(128)S(6)} %select_n.141, pred[1536]{0:T(1024)(128)(4,1)S(1)} %get-tuple-element.639, ...), kind=kOutput, calls=%fused_computation.99.clone.1 | convolution fusion | flops 209976832 | bytes 3682312 | tf_op jit(solution)/shard_map/while/body/eval_jaxpr/dot_general | solution.py:100
  183.4 3.3 %fusion.60 = (f32[512]{0:T(512)S(1)}, f32[512,1536]{1,0:T(8,128)S(1)}) fusion(f32[]{:T(128)} %bitcast.117, bf16[1536,256]{1,0:T(8,128)(2,1)} %get-tuple-element.633, s32[]{:T(128)S(6)} %select_n.143, bf16[512,1792]{1,0:T(8,128)(2,1)} %get-tuple-element.632, s32[]{:T(128)S(6)} %select_n.141, pred[1536]{0:T(1024)(128)(4,1)S(1)} %get-tuple-element.639, ...), kind=kOutput, calls=%fused_computation.99.clone.1 | convolution fusion | flops 209976832 | bytes 3682312 | tf_op jit(solution)/shard_map/while/body/eval_jaxpr/dot_general | solution.py:100
  196.6 3.3 %fusion.60 = (f32[512]{0:T(512)S(1)}, f32[512,1536]{1,0:T(8,128)S(1)}) fusion(f32[]{:T(128)} %bitcast.117, bf16[1536,256]{1,0:T(8,128)(2,1)} %get-tuple-element.633, s32[]{:T(128)S(6)} %select_n.143, bf16[512,1792]{1,0:T(8,128)(2,1)} %get-tuple-element.632, s32[]{:T(128)S(6)} %select_n.141, pred[1536]{0:T(1024)(128)(4,1)S(1)} %get-tuple-element.639, ...), kind=kOutput, calls=%fused_computation.99.clone.1 | convolution fusion | flops 209976832 | bytes 3682312 | tf_op jit(solution)/shard_map/while/body/eval_jaxpr/dot_general | solution.py:100
  209.9 3.3 %fusion.60 = (f32[512]{0:T(512)S(1)}, f32[512,1536]{1,0:T(8,128)S(1)}) fusion(f32[]{:T(128)} %bitcast.117, bf16[1536,256]{1,0:T(8,128)(2,1)} %get-tuple-element.633, s32[]{:T(128)S(6)} %select_n.143, bf16[512,1792]{1,0:T(8,128)(2,1)} %get-tuple-element.632, s32[]{:T(128)S(6)} %select_n.141, pred[1536]{0:T(1024)(128)(4,1)S(1)} %get-tuple-element.639, ...), kind=kOutput, calls=%fused_computation.99.clone.1 | convolution fusion | flops 209976832 | bytes 3682312 | tf_op jit(solution)/shard_map/while/body/eval_jaxpr/dot_general | solution.py:100
  214.6 2.8 multiply_reduce_fusion.2
  223.2 3.3 %fusion.60 = (f32[512]{0:T(512)S(1)}, f32[512,1536]{1,0:T(8,128)S(1)}) fusion(f32[]{:T(128)} %bitcast.117, bf16[1536,256]{1,0:T(8,128)(2,1)} %get-tuple-element.633, s32[]{:T(128)S(6)} %select_n.143, bf16[512,1792]{1,0:T(8,128)(2,1)} %get-tuple-element.632, s32[]{:T(128)S(6)} %select_n.141, pred[1536]{0:T(1024)(128)(4,1)S(1)} %get-tuple-element.639, ...), kind=kOutput, calls=%fused_computation.99.clone.1 | convolution fusion | flops 209976832 | bytes 3682312 | tf_op jit(solution)/shard_map/while/body/eval_jaxpr/dot_general | solution.py:100
  227.9 2.8 multiply_reduce_fusion.2
  236.6 3.3 %fusion.60 = (f32[512]{0:T(512)S(1)}, f32[512,1536]{1,0:T(8,128)S(1)}) fusion(f32[]{:T(128)} %bitcast.117, bf16[1536,256]{1,0:T(8,128)(2,1)} %get-tuple-element.633, s32[]{:T(128)S(6)} %select_n.143, bf16[512,1792]{1,0:T(8,128)(2,1)} %get-tuple-element.632, s32[]{:T(128)S(6)} %select_n.141, pred[1536]{0:T(1024)(128)(4,1)S(1)} %get-tuple-element.639, ...), kind=kOutput, calls=%fused_computation.99.clone.1 | convolution fusion | flops 209976832 | bytes 3682312 | tf_op jit(solution)/shard_map/while/body/eval_jaxpr/dot_general | solution.py:100
  241.2 2.8 multiply_reduce_fusion.2
  249.9 3.3 %fusion.60 = (f32[512]{0:T(512)S(1)}, f32[512,1536]{1,0:T(8,128)S(1)}) fusion(f32[]{:T(128)} %bitcast.117, bf16[1536,256]{1,0:T(8,128)(2,1)} %get-tuple-element.633, s32[]{:T(128)S(6)} %select_n.143, bf16[512,1792]{1,0:T(8,128)(2,1)} %get-tuple-element.632, s32[]{:T(128)S(6)} %select_n.141, pred[1536]{0:T(1024)(128)(4,1)S(1)} %get-tuple-element.639, ...), kind=kOutput, calls=%fused_computation.99.clone.1 | convolution fusion | flops 209976832 | bytes 3682312 | tf_op jit(solution)/shard_map/while/body/eval_jaxpr/dot_general | solution.py:100
  254.5 2.8 multiply_reduce_fusion.2
  263.2 3.3 %fusion.60 = (f32[512]{0:T(512)S(1)}, f32[512,1536]{1,0:T(8,128)S(1)}) fusion(f32[]{:T(128)} %bitcast.117, bf16[1536,256]{1,0:T(8,128)(2,1)} %get-tuple-element.633, s32[]{:T(128)S(6)} %select_n.143, bf16[512,1792]{1,0:T(8,128)(2,1)} %get-tuple-element.632, s32[]{:T(128)S(6)} %select_n.141, pred[1536]{0:T(1024)(128)(4,1)S(1)} %get-tuple-element.639, ...), kind=kOutput, calls=%fused_computation.99.clone.1 | convolution fusion | flops 209976832 | bytes 3682312 | tf_op jit(solution)/shard_map/while/body/eval_jaxpr/dot_general | solution.py:100
  267.9 2.8 multiply_reduce_fusion.2
  276.5 3.3 %fusion.60 = (f32[512]{0:T(512)S(1)}, f32[512,1536]{1,0:T(8,128)S(1)}) fusion(f32[]{:T(128)} %bitcast.117, bf16[1536,256]{1,0:T(8,128)(2,1)} %get-tuple-element.633, s32[]{:T(128)S(6)} %select_n.143, bf16[512,1792]{1,0:T(8,128)(2,1)} %get-tuple-element.632, s32[]{:T(128)S(6)} %select_n.141, pred[1536]{0:T(1024)(128)(4,1)S(1)} %get-tuple-element.639, ...), kind=kOutput, calls=%fused_computation.99.clone.1 | convolution fusion | flops 209976832 | bytes 3682312 | tf_op jit(solution)/shard_map/while/body/eval_jaxpr/dot_general | solution.py:100
  281.2 2.8 multiply_reduce_fusion.2
  294.3 10.3 %collective-permute-done.10 = bf16[2,512,256]{2,1,0:T(8,128)(2,1)S(1)} collective-permute-done((bf16[2,512,256]{2,1,0:T(8,128)(2,1)S(1)}, bf16[2,512,256]{2,1,0:T(8,128)(2,1)S(1)}, u32[]{:S(2)}, u32[]{:S(2)}) %collective-permute-start.10) | collective-permute-done | bytes 524320 | tf_op jit(solution)/shard_map/ppermute | solution.py:47
  304.6 6.1 %collective-permute-done.9 = bf16[2,512,256]{2,1,0:T(8,128)(2,1)S(1)} collective-permute-done((bf16[2,512,256]{2,1,0:T(8,128)(2,1)S(1)}, bf16[2,512,256]{2,1,0:T(8,128)(2,1)S(1)}, u32[]{:S(2)}, u32[]{:S(2)}) %collective-permute-start.9) | collective-permute-done | bytes 524320 | tf_op jit(solution)/shard_map/ppermute | solution.py:47
  (276 shorter events, 160.1 us)
Async XLA Ops:
  4.0 94.2 %collective-permute-start.1 = (bf16[2,512,256]{2,1,0:T(8,128)(2,1)}, bf16[2,512,256]{2,1,0:T(8,128)(2,1)}, u32[]{:S(2)}, u32[]{:S(2)}) collective-permute-start(bf16[2,512,256]{2,1,0:T(8,128)(2,1)} %constant_dynamic-update-slice_fusion), channel_id=1, source_target_pairs={{0,1},{1,2},{2,3},{3,4},{4,5},{5,6},{6,7},{8,9},{9,10},{10,11},{11... | collective-permute-start | bytes 1572872 | tf_op jit(solution)/shard_map/ppermute | solution.py:47
  7.8 91.5 %collective-permute-start = (bf16[2,512,256]{2,1,0:T(8,128)(2,1)}, bf16[2,512,256]{2,1,0:T(8,128)(2,1)}, u32[]{:S(2)}, u32[]{:S(2)}) collective-permute-start(bf16[2,512,256]{2,1,0:T(8,128)(2,1)} %constant_dynamic-update-slice_fusion), channel_id=1, source_target_pairs={{0,2},{1,3},{2,4},{3,5},{4,6},{5,7},{8,10},{9,11},{10,12},{11,13},... | collective-permute-start | bytes 1572872 | tf_op jit(solution)/shard_map/ppermute | solution.py:47
  16.6 5.0 %copy-start.7 = (s32[1,512]{1,0:T(1,128)S(1)}, s32[1,512]{1,0:T(1,128)}, u32[]{:S(2)}) copy-start(s32[1,512]{1,0:T(1,128)} %param.16) | copy-start | bytes 6148
  17.4 30.6 %collective-permute-start.2 = (bf16[1,512,224]{1,2,0:T(8,128)(2,1)}, bf16[1,512,224]{1,2,0:T(8,128)(2,1)}, u32[]{:S(2)}, u32[]{:S(2)}) collective-permute-start(bf16[1,512,224]{1,2,0:T(8,128)(2,1)} %bitcast.109), channel_id=1, source_target_pairs={{0,1},{1,0},{2,3},{3,2},{4,5},{5,4},{6,7},{7,6},{8,9},{9,8},{10,11... | collective-permute-start | bytes 688136 | tf_op jit(solution)/shard_map/ppermute | solution.py:37
  18.5 35.8 %collective-permute-start.3 = (bf16[1,512,224]{1,2,0:T(8,128)(2,1)}, bf16[1,512,224]{1,2,0:T(8,128)(2,1)}, u32[]{:S(2)}, u32[]{:S(2)}) collective-permute-start(bf16[1,512,224]{1,2,0:T(8,128)(2,1)} %bitcast.108), channel_id=1, source_target_pairs={{0,2},{1,3},{2,0},{3,1},{4,6},{5,7},{6,4},{7,5},{8,10},{9,11},{10,... | collective-permute-start | bytes 688136 | tf_op jit(solution)/shard_map/ppermute | solution.py:37
  19.2 36.7 %collective-permute-start.4 = (bf16[1,512,224]{1,2,0:T(8,128)(2,1)}, bf16[1,512,224]{1,2,0:T(8,128)(2,1)S(1)}, u32[]{:S(2)}, u32[]{:S(2)}) collective-permute-start(bf16[1,512,224]{1,2,0:T(8,128)(2,1)} %bitcast.107), channel_id=1, source_target_pairs={{0,3},{1,2},{2,1},{3,0},{4,7},{5,6},{6,5},{7,4},{8,11},{9,10},{10,... | collective-permute-start | bytes 688136 | tf_op jit(solution)/shard_map/ppermute | solution.py:37
  46.6 9.3 %copy-start.6 = (bf16[1,1,512,224]{2,3,0,1:T(8,128)(2,1)S(1)}, bf16[1,1,512,224]{2,3,0,1:T(8,128)(2,1)}, u32[]{:S(2)}) copy-start(bf16[1,1,512,224]{2,3,0,1:T(8,128)(2,1)} %copy.47) | copy-start | bytes 688132
  46.6 24.2 %copy-start.5 = (bf16[1,1,512,224]{2,3,0,1:T(8,128)(2,1)S(1)}, bf16[1,1,512,224]{2,3,0,1:T(8,128)(2,1)}, u32[]{:S(2)}) copy-start(bf16[1,1,512,224]{2,3,0,1:T(8,128)(2,1)} %copy.46) | copy-start | bytes 688132
  48.0 22.8 %collective-permute-start.5 = (bf16[1,512,224]{1,2,0:T(8,128)(2,1)S(1)}, bf16[1,512,224]{1,2,0:T(8,128)(2,1)S(1)}, u32[]{:S(2)}, u32[]{:S(2)}) collective-permute-start(bf16[1,512,224]{1,2,0:T(8,128)(2,1)S(1)} %bitcast.134), channel_id=1, source_target_pairs={{0,4},{1,5},{2,6},{3,7},{4,0},{5,1},{6,2},{7,3},{8,12},{9,13},{10,... | collective-permute-start | bytes 688136 | tf_op jit(solution)/shard_map/ppermute | solution.py:37
  54.3 21.5 %collective-permute-start.6 = (bf16[1,512,224]{1,2,0:T(8,128)(2,1)}, bf16[1,512,224]{1,2,0:T(8,128)(2,1)S(1)}, u32[]{:S(2)}, u32[]{:S(2)}) collective-permute-start(bf16[1,512,224]{1,2,0:T(8,128)(2,1)} %bitcast.133), channel_id=1, source_target_pairs={{0,5},{1,4},{2,7},{3,6},{4,1},{5,0},{6,3},{7,2},{8,13},{9,12},{10,... | collective-permute-start | bytes 688136 | tf_op jit(solution)/shard_map/ppermute | solution.py:37
  55.9 31.6 %collective-permute-start.7 = (bf16[1,512,224]{1,2,0:T(8,128)(2,1)S(1)}, bf16[1,512,224]{1,2,0:T(8,128)(2,1)S(1)}, u32[]{:S(2)}, u32[]{:S(2)}) collective-permute-start(bf16[1,512,224]{1,2,0:T(8,128)(2,1)S(1)} %bitcast.132), channel_id=1, source_target_pairs={{0,6},{1,7},{2,4},{3,5},{4,2},{5,3},{6,0},{7,1},{8,14},{9,15},{10,... | collective-permute-start | bytes 688136 | tf_op jit(solution)/shard_map/ppermute | solution.py:37
  70.8 21.6 %collective-permute-start.8 = (bf16[1,512,224]{1,2,0:T(8,128)(2,1)S(1)}, bf16[1,512,224]{1,2,0:T(8,128)(2,1)S(1)}, u32[]{:S(2)}, u32[]{:S(2)}) collective-permute-start(bf16[1,512,224]{1,2,0:T(8,128)(2,1)S(1)} %bitcast.131), channel_id=1, source_target_pairs={{0,7},{1,6},{2,5},{3,4},{4,3},{5,2},{6,1},{7,0},{8,15},{9,14},{10,... | collective-permute-start | bytes 688136 | tf_op jit(solution)/shard_map/ppermute | solution.py:37
  98.1 2.2 copy-start.2
  98.1 2.2 copy-start.3
  101.7 1.5 copy-start.8
  113.2 1.6 copy-start
  126.5 1.6 copy-start
  133.6 1.4 copy-start.4
  139.7 1.6 copy-start
  153.0 1.6 copy-start
  166.2 1.6 copy-start
  179.5 1.6 copy-start
  192.7 1.6 copy-start
  206.0 1.6 copy-start
  219.3 1.6 copy-start
  232.6 1.6 copy-start
  246.0 1.6 copy-start
  259.3 1.6 copy-start
  272.6 1.6 copy-start
  285.9 1.6 copy-start
  289.5 15.1 %collective-permute-start.10 = (bf16[2,512,256]{2,1,0:T(8,128)(2,1)S(1)}, bf16[2,512,256]{2,1,0:T(8,128)(2,1)S(1)}, u32[]{:S(2)}, u32[]{:S(2)}) collective-permute-start(bf16[2,512,256]{2,1,0:T(8,128)(2,1)S(1)} %pad_maximum_fusion.3), channel_id=1, source_target_pairs={{2,0},{3,1},{4,2},{5,3},{6,4},{7,5},{10,8},{11,9},{12,10},{13,11},... | collective-permute-start | bytes 1572872 | tf_op jit(solution)/shard_map/ppermute | solution.py:47
  291.7 19.0 %collective-permute-start.9 = (bf16[2,512,256]{2,1,0:T(8,128)(2,1)S(1)}, bf16[2,512,256]{2,1,0:T(8,128)(2,1)S(1)}, u32[]{:S(2)}, u32[]{:S(2)}) collective-permute-start(bf16[2,512,256]{2,1,0:T(8,128)(2,1)S(1)} %pad_maximum_fusion.2), channel_id=1, source_target_pairs={{1,0},{2,1},{3,2},{4,3},{5,4},{6,5},{7,6},{9,8},{10,9},{11,10},{12... | collective-permute-start | bytes 1572872 | tf_op jit(solution)/shard_map/ppermute | solution.py:47
  (14 other events, 19.1 us)
